TPU v7x, 256 devices: a whole 4x4x8 slice. The times are simulated.
256 devices in a mesh: row: 16 (over x_lo, z), col: 16 (over x_hi, y, core).
Axes of the slice: x: 4 (x_hi: 2, x_lo: 2; x = x_hi * 2 + x_lo), y: 4, z: 8, core: 2. Of those that a mesh axis runs over, the one named last changes fastest.
Arguments:
- tensor: bfloat16 [4096, 2048, 128], P('row', 'col'), may hold values from -96 to 96
- factor_a: float32 [4096, 128], P(('row', 'col')), may hold values from -4.5 to 4.5
- factor_b: float32 [2048, 128], P(('col', 'row')), may hold values from -4.5 to 4.5
- factor_c: float32 [128, 128], replicated, may hold values from -4.5 to 4.5
Outputs:
- new_a: float32 [4096, 128], P(('row', 'col'))
- new_b: float32 [2048, 128], P(('col', 'row'))
- new_c: float32 [128, 128], replicated
All inputs are finite; a program needn't handle non-finite values.
Results may differ from a plain program's by a relative error of at most 0.01.
Values may be sent and summed in bfloat16 or wider, within the bound.
A program may use at most 128 MiB of HBM per device.

v0:
```python
import jax
import jax.numpy as jnp
from jax import lax
from jax.sharding import PartitionSpec as P

STEPS = 2
damping = 0.9
scaling = 0.25
epsilon = 1e-06


def column_squares(values16):
    return jnp.sum(jnp.square(values16.astype(jnp.float32)), axis=0)


def local_terms(block, tile_a, tile_b, c16):
    rows_i, rows_j, depth = block.shape
    rank = tile_a.shape[1]
    pairs = (
        tile_a.astype(jnp.float32)[:, None, :] * tile_b.astype(jnp.float32)[None, :, :]
    ).astype(jnp.bfloat16)
    pairs = pairs.reshape(rows_i * rows_j, rank)
    model = jnp.dot(pairs, c16.T, preferred_element_type=jnp.float32)
    resid = (block.reshape(rows_i * rows_j, depth).astype(jnp.float32) - model).astype(jnp.bfloat16)
    along = jnp.dot(resid, c16, preferred_element_type=jnp.float32).reshape(rows_i, rows_j, rank)
    grad_a = jnp.sum(along * tile_b.astype(jnp.float32)[None, :, :], axis=1)
    grad_b = jnp.sum(along * tile_a.astype(jnp.float32)[:, None, :], axis=0)
    grad_c = lax.dot_general(
        resid, pairs, (((0,), (0,)), ((), ())), preferred_element_type=jnp.float32
    )
    return (grad_a, grad_b, grad_c)


def local(tensor, factor_a, factor_b, factor_c):
    own_a, own_b, third = (factor_a, factor_b, factor_c)
    for step in range(STEPS):
        a_mine16 = own_a.astype(jnp.bfloat16)
        b_mine16 = own_b.astype(jnp.bfloat16)
        tile_a = lax.all_gather(a_mine16, "col", axis=0, tiled=True)
        tile_b = lax.all_gather(b_mine16, "row", axis=0, tiled=True)
        norm_a, norm_b = lax.psum(
            (column_squares(a_mine16), column_squares(b_mine16)), ("row", "col")
        )
        c16 = third.astype(jnp.bfloat16)
        norm_c = column_squares(c16)
        step_a = scaling / (norm_b * norm_c + epsilon)
        step_b = scaling / (norm_a * norm_c + epsilon)
        step_c = scaling / (norm_a * norm_b + epsilon)
        grad_a, grad_b, grad_c = local_terms(tensor, tile_a, tile_b, c16)
        grad_a = lax.psum_scatter(
            grad_a.astype(jnp.bfloat16), "col", scatter_dimension=0, tiled=True
        ).astype(jnp.float32)
        grad_b = lax.psum_scatter(
            grad_b.astype(jnp.bfloat16), "row", scatter_dimension=0, tiled=True
        ).astype(jnp.float32)
        own_a = damping * own_a + step_a * grad_a
        own_b = damping * own_b + step_b * grad_b
        grad_c = lax.psum(grad_c, ("row", "col"))
        third = damping * third + step_c * grad_c
    return (own_a, own_b, third)


def solution(mesh):
    return jax.shard_map(
        local,
        mesh=mesh,
        in_specs=(P("row", "col", None), P(("row", "col"), None), P(("col", "row"), None), P()),
        out_specs=(P(("row", "col"), None), P(("col", "row"), None), P()),
        check_vma=False,
    )
```

profile of v0, /device:TPU:1, one launch (start us, length us, event | category | flops | bytes accessed | tf_op | source)
XLA Modules:
  0.0 663.4 jit_solution(11993279583761159699)
XLA Ops:
  9.5 30.3 %all_gather.13 = bf16[128,128]{1,0:T(8,128)(2,1)S(1)} all-gather(bf16[8,128]{1,0:T(8,128)(2,1)S(1)} %get-tuple-element.14), channel_id=1, replica_groups=mesh['row'=16,'col'=16] {'row'}, dimensions={0}, use_global_device_ids=true | all-gather | bytes 34816 | tf_op jit(solution)/shard_map/all_gather | solution.py:40
  39.8 31.7 %all_gather.12 = bf16[256,128]{1,0:T(8,128)(2,1)S(1)} all-gather(bf16[16,128]{1,0:T(8,128)(2,1)S(1)} %get-tuple-element.16), channel_id=1, replica_groups=mesh['row'=16,'col'=16] {'col'}, dimensions={0}, use_global_device_ids=true | all-gather | bytes 69632 | tf_op jit(solution)/shard_map/all_gather | solution.py:39
  71.5 5.6 multiply_convert_fusion.1
  77.1 8.1 %fusion.1 = bf16[32768,128]{1,0:T(8,128)(2,1)S(1)} fusion(bf16[32768,128]{1,0:T(8,128)(2,1)} %bitcast.21, bf16[32768,128]{1,0:T(8,128)(2,1)} %bitcast.25, f32[128,128]{1,0:T(8,128)S(1)} %copy-done.2), kind=kOutput, calls=%fused_computation.3 | convolution fusion | flops 1086341120 | bytes 25231360 | tf_op jit(solution)/shard_map/dot_general | solution.py:23
  85.2 3.2 copy-done
  88.5 6.4 fusion.11
  94.9 12.1 %multiply_reduce_fusion.3 = (bf16[256,128]{1,0:T(8,128)(2,1)}, f32[32768,128]{1,0:T(8,128)}) fusion(f32[128,128]{1,0:T(8,128)S(1)} %convert_element_type.111, bf16[32768,128]{1,0:T(8,128)(2,1)} %copy-done, f32[128,128]{1,0:T(8,128)S(1)} %copy-done.2), kind=kOutput, calls=%fused_computation.8 | convolution fusion | flops 1082114048 | bytes 25362432 | tf_op jit(solution)/shard_map/dot_general | solution.py:25
  107.1 7.3 %multiply_reduce_fusion.2 = bf16[128,128]{1,0:T(8,128)(2,1)S(1)} fusion(f32[256,128,128]{2,1,0:T(8,128)} %bitcast.23, f32[256,128]{1,0:T(8,128)S(1)} %convert_element_type.110), kind=kLoop, calls=%fused_computation.7 | loop fusion | flops 8372224 | bytes 16941056 | tf_op jit(solution)/shard_map/reduce_sum | solution.py:27
  114.5 46.3 %all-reduce = bf16[128,128]{1,0:T(8,128)(2,1)S(1)} all-reduce(bf16[128,128]{1,0:T(8,128)(2,1)S(1)} %multiply_reduce_fusion.2), channel_id=3, replica_groups=mesh['row'=16,'col'=16] {'row'}, use_global_device_ids=true, to_apply=%region_8.0.clone | all-reduce | flops 16384 | bytes 65536
  162.0 84.4 %all-reduce.3 = (f32[128]{0:T(128)S(1)}, f32[128]{0:T(128)S(1)}) all-reduce(f32[128]{0:T(128)S(1)} %get-tuple-element.15, f32[128]{0:T(128)S(1)} %get-tuple-element.13), channel_id=1, replica_groups=mesh['row'=16,'col'=16] {'row','col'}, use_global_device_ids=true, to_apply=%region_6.0 | all-reduce | flops 256 | bytes 2048 | tf_op jit(solution)/shard_map/psum | solution.py:41
  246.4 81.7 %all-reduce.7.cloned.1.call-done = f32[128,128]{1,0:T(8,128)} async-done(((f32[128,128]{1,0:T(8,128)}), f32[128,128]{1,0:T(8,128)}) %all-reduce.7.cloned.1.call-update) | async-done | bytes 65552 | tf_op jit(solution)/shard_map/psum | solution.py:58
  329.1 24.4 %all_gather.15 = bf16[128,128]{1,0:T(8,128)(2,1)S(1)} all-gather(bf16[8,128]{1,0:T(8,128)(2,1)S(1)} %get-tuple-element.12), channel_id=1, replica_groups=mesh['row'=16,'col'=16] {'row'}, dimensions={0}, use_global_device_ids=true | all-gather | bytes 34816 | tf_op jit(solution)/shard_map/all_gather | solution.py:40
  354.2 28.8 %all_gather.14 = bf16[256,128]{1,0:T(8,128)(2,1)S(1)} all-gather(bf16[16,128]{1,0:T(8,128)(2,1)S(1)} %get-tuple-element.10), channel_id=1, replica_groups=mesh['row'=16,'col'=16] {'col'}, dimensions={0}, use_global_device_ids=true | all-gather | bytes 69632 | tf_op jit(solution)/shard_map/all_gather | solution.py:39
  383.0 5.6 multiply_convert_fusion
  388.6 8.1 %fusion = bf16[32768,128]{1,0:T(8,128)(2,1)S(1)} fusion(bf16[32768,128]{1,0:T(8,128)(2,1)} %bitcast.19, bf16[128,128]{1,0:T(8,128)(2,1)S(1)} %get-tuple-element.8, bf16[32768,128]{1,0:T(8,128)(2,1)} %bitcast.26), kind=kOutput, calls=%fused_computation.1 | convolution fusion | flops 1086324736 | bytes 25198592 | tf_op jit(solution)/shard_map/dot_general | solution.py:23
  396.8 3.2 copy-done.1
  400.0 6.4 fusion.12
  406.4 12.1 %multiply_reduce_fusion.1 = (bf16[256,128]{1,0:T(8,128)(2,1)}, f32[32768,128]{1,0:T(8,128)}) fusion(f32[128,128]{1,0:T(8,128)S(1)} %convert_element_type.126, bf16[32768,128]{1,0:T(8,128)(2,1)} %copy-done.1, bf16[128,128]{1,0:T(8,128)(2,1)S(1)} %get-tuple-element.8), kind=kOutput, calls=%fused_computation.5 | convolution fusion | flops 1082097664 | bytes 25329664 | tf_op jit(solution)/shard_map/dot_general | solution.py:25
  418.5 7.3 %multiply_reduce_fusion = bf16[128,128]{1,0:T(8,128)(2,1)S(1)} fusion(f32[256,128,128]{2,1,0:T(8,128)} %bitcast.24, f32[256,128]{1,0:T(8,128)S(1)} %convert_element_type.125), kind=kLoop, calls=%fused_computation.4 | loop fusion | flops 8372224 | bytes 16941056 | tf_op jit(solution)/shard_map/reduce_sum | solution.py:27
  425.8 47.7 %all-reduce.1 = bf16[128,128]{1,0:T(8,128)(2,1)S(1)} all-reduce(bf16[128,128]{1,0:T(8,128)(2,1)S(1)} %multiply_reduce_fusion), channel_id=5, replica_groups=mesh['row'=16,'col'=16] {'row'}, use_global_device_ids=true, to_apply=%region_18.0.clone | all-reduce | flops 16384 | bytes 65536
  473.5 86.2 %all-reduce.2 = (f32[128]{0:T(128)S(1)}, f32[128]{0:T(128)S(1)}) all-reduce(f32[128]{0:T(128)S(1)} %get-tuple-element.11, f32[128]{0:T(128)S(1)} %get-tuple-element.9), channel_id=1, replica_groups=mesh['row'=16,'col'=16] {'row','col'}, use_global_device_ids=true, to_apply=%region_10.0 | all-reduce | flops 256 | bytes 2048 | tf_op jit(solution)/shard_map/psum | solution.py:41
  560.3 92.8 %all-reduce.9.cloned.1.call-done = f32[128,128]{1,0:T(8,128)} async-done(((f32[128,128]{1,0:T(8,128)}), f32[128,128]{1,0:T(8,128)}) %all-reduce.9.cloned.1.call-update) | async-done | bytes 65552 | tf_op jit(solution)/shard_map/psum | solution.py:58
  653.2 1.5 multiply_add_fusion
  654.6 1.3 multiply_add_fusion.2
  (38 shorter events, 4.6 us)
Async XLA Ops:
  8.0 69.1 %copy-start.2 = (f32[128,128]{1,0:T(8,128)S(1)}, f32[128,128]{1,0:T(8,128)}, u32[]{:S(2)}) copy-start(f32[128,128]{1,0:T(8,128)} %param.7) | copy-start | bytes 196612
  8.0 320.1 %all-reduce.7.cloned.1.call-start = ((), (), s32[]{:S(2)}) async-start(), calls=%async_computation.3 | async-start | bytes 131072 | tf_op jit(solution)/shard_map/psum | solution.py:58
  85.2 3.2 copy-start
  94.9 258.6 %reduce-scatter.3.cloned.1.call-start = ((), (), s32[]{:S(2)}) async-start(), calls=%async_computation.2 | async-start | bytes 69632 | tf_op jit(solution)/shard_map/reduce_scatter | solution.py:50
  107.0 546.1 %all-reduce.9.cloned.1.call-start = ((), (), s32[]{:S(2)}) async-start(), calls=%async_computation.5 | async-start | bytes 131072 | tf_op jit(solution)/shard_map/psum | solution.py:58
  107.1 53.7 %copy-start.7 = (u32[256]{0:T(256)S(1)}, u32[256]{0:T(256)}, u32[]{:S(2)}) copy-start(u32[256]{0:T(256)} %constant.14) | copy-start | bytes 3076
  107.1 221.9 %copy-start.5 = (f32[8,128]{1,0:T(8,128)S(1)}, f32[8,128]{1,0:T(8,128)}, u32[]{:S(2)}) copy-start(f32[8,128]{1,0:T(8,128)} %param.6) | copy-start | bytes 12292
  107.1 246.4 %copy-start.4 = (f32[16,128]{1,0:T(8,128)S(1)}, f32[16,128]{1,0:T(8,128)}, u32[]{:S(2)}) copy-start(f32[16,128]{1,0:T(8,128)} %param.5) | copy-start | bytes 24580
  396.7 3.2 copy-start.1
  418.4 236.2 %reduce-scatter.5.cloned.1.call-start = ((), (), s32[]{:S(2)}) async-start(), calls=%async_computation.4 | async-start | bytes 69632 | tf_op jit(solution)/shard_map/reduce_scatter | solution.py:50
  418.5 234.7 %copy-start.3 = (f32[128,128]{1,0:T(8,128)S(1)}, f32[128,128]{1,0:T(8,128)}, u32[]{:S(2)}) copy-start(f32[128,128]{1,0:T(8,128)} %all-reduce.7.cloned.1.call-done) | copy-start | bytes 196612
  418.5 236.1 %copy-start.6 = (bf16[16,128]{1,0:T(8,128)(2,1)S(1)}, bf16[16,128]{1,0:T(8,128)(2,1)}, u32[]{:S(2)}) copy-start(bf16[16,128]{1,0:T(8,128)(2,1)} %reduce-scatter.3.cloned.1.call-done) | copy-start | bytes 12292
Sparse Core Ops, SparseCore 0:
  95.0 233.1 all-reduce.6
  418.6 234.5 all-reduce.8
Sparse Core Ops, SparseCore 1:
  107.1 58.3 reduce-scatter.2
  560.4 60.9 reduce-scatter.4
where the time goes:
time: 664 us; the launch traced here: 663 us
  blocking collectives  380 us (57%)
  waiting for transfers between devices  175 us (26%)
  matrix products  53.2 us (8%)
  other arithmetic  32.4 us (5%)
  between operations  16.3 us (2%)
  local copies, waits for them, and re-layouts  7.04 us (1%)
    psum x2, waiting for transfers between devices, local(): grad_c = lax.psum(grad_c, ('row', 'col'))  175 us
    psum x2, blocking collectives, local(): lax.psum((column_squares(a_mine16), column_squares(b_mine16)), ('row', 'c...  171 us
    unnamed x2, blocking collectives  94 us
    all_gather x2, blocking collectives, local(): tile_a = lax.all_gather(a_mine16, 'col', axis=0, tiled=True)  60.5 us
    all_gather x2, blocking collectives, local(): tile_b = lax.all_gather(b_mine16, 'row', axis=0, tiled=True)  54.7 us
    dot_general x2, matrix products, local_terms(): jnp.dot(resid, c16, preferred_element_type=jnp.float32)  24.1 us
    dot_general x2, matrix products, local_terms(): model = jnp.dot(pairs, c16.T, preferred_element_type=jnp.float32)  16.2 us
    reduce_sum x2, other arithmetic, local_terms(): grad_b = jnp.sum(along * tile_a.astype(jnp.float32)[:, None, :], axis=0)  14.7 us
  transfers between devices with their start and end apart: 4, of which 2 were waited for; matrix products, arithmetic and copies ran while one was open for 5% of the time, Pallas kernels for 0%

commit v1 on v0

--- a/solution.py
+++ b/solution.py
@@ -55,7 +55,7 @@
         ).astype(jnp.float32)
         own_a = damping * own_a + step_a * grad_a
         own_b = damping * own_b + step_b * grad_b
-        grad_c = lax.psum(grad_c, ("row", "col"))
+        grad_c = jnp.sum(lax.all_gather(grad_c, ("row", "col")), axis=0)
         third = damping * third + step_c * grad_c
     return (own_a, own_b, third)
 

time: 664 us -> 1040 us (1.57)
  waiting for transfers between devices: 175 us -> 553 us
  blocking collectives: 380 us -> 368 us
    all_gather x0 -> x2, waiting for transfers between devices: none -> 552 us  [local(): grad_c = jnp.sum(lax.all_gather(grad_c, ('row', 'col')), axis=0)]
    psum x2 -> x0, waiting for transfers between devices: 175 us -> none  [local(): grad_c = lax.psum(grad_c, ('row', 'col'))]
    reduce_sum x0 -> x2, other arithmetic: none -> 13.2 us  [local(): grad_c = jnp.sum(lax.all_gather(grad_c, ('row', 'col')), axis=0)]
    psum x2, blocking collectives: 171 us -> 158 us  [local(): lax.psum((column_squares(a_mine16), column_squares(b_mine16)), ('row', 'c...]
  transfers between devices with their start and end apart: 4 -> 4, of which waited for: 2 -> 2; matrix products, arithmetic and copies ran while one was open for 5% -> 4% of each run, Pallas kernels for 0% -> 0%
where the time goes in v1:
time: 1040 us
  waiting for transfers between devices  553 us (53%)
  blocking collectives  368 us (35%)
  matrix products  57.2 us (6%)
  other arithmetic  40.8 us (4%)
  between operations  16.3 us (2%)
    all_gather x2, waiting for transfers between devices, local(): grad_c = jnp.sum(lax.all_gather(grad_c, ('row', 'col')), axis=0)  552 us
    psum x2, blocking collectives, local(): lax.psum((column_squares(a_mine16), column_squares(b_mine16)), ('row', 'c...  158 us
    unnamed x2, blocking collectives  94.2 us
    all_gather x2, blocking collectives, local(): tile_a = lax.all_gather(a_mine16, 'col', axis=0, tiled=True)  61.8 us
    all_gather x2, blocking collectives, local(): tile_b = lax.all_gather(b_mine16, 'row', axis=0, tiled=True)  54.2 us
    dot_general x2, matrix products, local_terms(): jnp.dot(resid, c16, preferred_element_type=jnp.float32)  24.2 us
  transfers between devices with their start and end apart: 4, of which 2 were waited for; matrix products, arithmetic and copies ran while one was open for 4% of the time, Pallas kernels for 0%

profile of v1, /device:TPU:1, one launch (start us, length us, event | category | flops | bytes accessed | tf_op | source)
XLA Modules:
  0.0 1038.6 jit_solution(1769423632100732661)
XLA Ops:
  9.5 30.3 %all_gather.25 = bf16[128,128]{1,0:T(8,128)(2,1)S(1)} all-gather(bf16[8,128]{1,0:T(8,128)(2,1)S(1)} %get-tuple-element.14), channel_id=1, replica_groups=mesh['row'=16,'col'=16] {'row'}, dimensions={0}, use_global_device_ids=true | all-gather | bytes 34816 | tf_op jit(solution)/shard_map/all_gather | solution.py:40
  39.8 31.7 %all_gather.24 = bf16[256,128]{1,0:T(8,128)(2,1)S(1)} all-gather(bf16[16,128]{1,0:T(8,128)(2,1)S(1)} %get-tuple-element.16), channel_id=1, replica_groups=mesh['row'=16,'col'=16] {'col'}, dimensions={0}, use_global_device_ids=true | all-gather | bytes 69632 | tf_op jit(solution)/shard_map/all_gather | solution.py:39
  71.5 5.6 multiply_convert_fusion.1
  77.1 8.1 fusion.1
  85.2 3.2 copy-done.1
  88.4 6.4 fusion.11
  94.9 12.1 %multiply_reduce_fusion.3 = (bf16[256,128]{1,0:T(8,128)(2,1)}, f32[32768,128]{1,0:T(8,128)}) fusion(f32[128,128]{1,0:T(8,128)S(1)} %convert_element_type.111, bf16[32768,128]{1,0:T(8,128)(2,1)} %copy-done.1, f32[128,128]{1,0:T(8,128)S(1)} %copy-done.2), kind=kOutput, calls=%fused_computation.8 | convolution fusion | flops 1082114048 | bytes 25362432 | tf_op jit(solution)/shard_map/dot_general | solution.py:25
  107.1 7.4 multiply_reduce_fusion.2
  114.5 46.3 %all-reduce = bf16[128,128]{1,0:T(8,128)(2,1)S(1)} all-reduce(bf16[128,128]{1,0:T(8,128)(2,1)S(1)} %multiply_reduce_fusion.2), channel_id=5, replica_groups=mesh['row'=16,'col'=16] {'row'}, use_global_device_ids=true, to_apply=%region_8.0.clone | all-reduce | flops 16384 | bytes 65536
  162.0 84.8 %all-reduce.3 = (f32[128]{0:T(128)S(1)}, f32[128]{0:T(128)S(1)}) all-reduce(f32[128]{0:T(128)S(1)} %get-tuple-element.15, f32[128]{0:T(128)S(1)} %get-tuple-element.13), channel_id=1, replica_groups=mesh['row'=16,'col'=16] {'row','col'}, use_global_device_ids=true, to_apply=%region_6.0 | all-reduce | flops 256 | bytes 2048 | tf_op jit(solution)/shard_map/psum | solution.py:41
  246.8 264.6 %all-gather.5.cloned.1.call-done = f32[32768,128]{1,0:T(8,128)} async-done(((f32[128,128]{1,0:T(8,128)}), f32[32768,128]{1,0:T(8,128)}) %all-gather.5.cloned.1.call-update) | async-done | bytes 16777232 | tf_op jit(solution)/shard_map/all_gather | solution.py:58
  511.5 6.6 reduce_sum.114
  518.2 24.0 %all_gather.29 = bf16[128,128]{1,0:T(8,128)(2,1)S(1)} all-gather(bf16[8,128]{1,0:T(8,128)(2,1)S(1)} %get-tuple-element.12), channel_id=1, replica_groups=mesh['row'=16,'col'=16] {'row'}, dimensions={0}, use_global_device_ids=true | all-gather | bytes 34816 | tf_op jit(solution)/shard_map/all_gather | solution.py:40
  542.9 30.0 %all_gather.28 = bf16[256,128]{1,0:T(8,128)(2,1)S(1)} all-gather(bf16[16,128]{1,0:T(8,128)(2,1)S(1)} %get-tuple-element.10), channel_id=1, replica_groups=mesh['row'=16,'col'=16] {'col'}, dimensions={0}, use_global_device_ids=true | all-gather | bytes 69632 | tf_op jit(solution)/shard_map/all_gather | solution.py:39
  572.9 2.4 multiply_convert_fusion
  575.3 9.7 fusion
  585.1 12.1 %multiply_reduce_fusion.1 = (bf16[256,128]{1,0:T(8,128)(2,1)}, f32[32768,128]{1,0:T(8,128)}) fusion(f32[128,128]{1,0:T(8,128)S(1)} %convert_element_type.126, bf16[32768,128]{1,0:T(8,128)(2,1)} %fusion, bf16[128,128]{1,0:T(8,128)(2,1)S(1)} %get-tuple-element.8), kind=kOutput, calls=%fused_computation.5 | convolution fusion | flops 1082097664 | bytes 25329664 | tf_op jit(solution)/shard_map/dot_general | solution.py:25
  597.2 8.8 fusion.12
  606.0 72.9 %all-reduce.2 = (f32[128]{0:T(128)S(1)}, f32[128]{0:T(128)S(1)}) all-reduce(f32[128]{0:T(128)S(1)} %get-tuple-element.11, f32[128]{0:T(128)S(1)} %get-tuple-element.9), channel_id=1, replica_groups=mesh['row'=16,'col'=16] {'row','col'}, use_global_device_ids=true, to_apply=%region_10.0 | all-reduce | flops 256 | bytes 2048 | tf_op jit(solution)/shard_map/psum | solution.py:41
  678.9 7.4 multiply_reduce_fusion
  686.3 47.9 %all-reduce.1 = bf16[128,128]{1,0:T(8,128)(2,1)S(1)} all-reduce(bf16[128,128]{1,0:T(8,128)(2,1)S(1)} %multiply_reduce_fusion), channel_id=7, replica_groups=mesh['row'=16,'col'=16] {'row'}, use_global_device_ids=true, to_apply=%region_18.0.clone | all-reduce | flops 16384 | bytes 65536
  734.8 1.3 multiply_add_fusion.2
  736.1 287.8 %all-gather.7.cloned.1.call-done = f32[32768,128]{1,0:T(8,128)} async-done(((f32[128,128]{1,0:T(8,128)}), f32[32768,128]{1,0:T(8,128)}) %all-gather.7.cloned.1.call-update) | async-done | bytes 16777232 | tf_op jit(solution)/shard_map/all_gather | solution.py:58
  1023.9 6.6 reduce_sum.119
  (38 shorter events, 4.4 us)
Async XLA Ops:
  8.0 69.1 %copy-start.2 = (f32[128,128]{1,0:T(8,128)S(1)}, f32[128,128]{1,0:T(8,128)}, u32[]{:S(2)}) copy-start(f32[128,128]{1,0:T(8,128)} %param.7) | copy-start | bytes 196612
  8.0 503.5 %all-gather.5.cloned.1.call-start = ((), (), s32[]{:S(2)}) async-start(), calls=%async_computation.4 | async-start | bytes 16842752 | tf_op jit(solution)/shard_map/all_gather | solution.py:58
  85.2 3.2 copy-start.1
  94.8 447.3 %reduce-scatter.3.cloned.1.call-start = ((), (), s32[]{:S(2)}) async-start(), calls=%async_computation.2 | async-start | bytes 69632 | tf_op jit(solution)/shard_map/reduce_scatter | solution.py:50
  107.0 627.8 %reduce-scatter.5.cloned.1.call-start = ((), (), s32[]{:S(2)}) async-start(), calls=%async_computation.3 | async-start | bytes 69632 | tf_op jit(solution)/shard_map/reduce_scatter | solution.py:50
  107.1 53.7 %copy-start.6 = (u32[256]{0:T(256)S(1)}, u32[256]{0:T(256)}, u32[]{:S(2)}) copy-start(u32[256]{0:T(256)} %constant.14) | copy-start | bytes 3076
  511.5 6.7 copy-start.4
  511.5 30.7 %copy-start.3 = (f32[16,128]{1,0:T(8,128)S(1)}, f32[16,128]{1,0:T(8,128)}, u32[]{:S(2)}) copy-start(f32[16,128]{1,0:T(8,128)} %param.5) | copy-start | bytes 24580
  575.3 9.7 copy-start
  597.2 426.8 %all-gather.7.cloned.1.call-start = ((), (), s32[]{:S(2)}) async-start(), calls=%async_computation.5 | async-start | bytes 16842752 | tf_op jit(solution)/shard_map/all_gather | solution.py:58
  678.9 55.9 %copy-start.5 = (bf16[16,128]{1,0:T(8,128)(2,1)S(1)}, bf16[16,128]{1,0:T(8,128)(2,1)}, u32[]{:S(2)}) copy-start(bf16[16,128]{1,0:T(8,128)(2,1)} %reduce-scatter.3.cloned.1.call-done) | copy-start | bytes 12292
Sparse Core Ops, SparseCore 0:
  95.0 416.4 all-gather.4
  606.2 417.7 all-gather.6
Sparse Core Ops, SparseCore 1:
  107.1 58.3 reduce-scatter.2
  597.2 59.4 reduce-scatter.4
